TPU v7x, 32 devices: a whole 2x2x4 slice. The times are simulated.
32 devices in a mesh: noise: 8 (over z, y), tile: 4 (over x, core).
Axes of the slice: x: 2, y: 2, z: 4, core: 2. Of those that a mesh axis runs over, the one named last changes fastest.
Arguments:
- queue_state: float32 [32, 69, 4, 256], P('noise', None, 'tile'), may hold values from -6 to 6
- fresh_noise: float32 [2, 69, 4, 256], P(None, None, 'tile'), may hold values from -6 to 6
- plan: float32 [17], replicated, may hold values from 0.5 to 2
- levels: int32 [32], P('noise'), may hold values from 0 to 15
- neighbours: int32 [4, 4], replicated, may hold values from -1 to 3, as said below
- in_weight: bfloat16 [256, 69], replicated, may hold values from -0.75 to 0.75
- level_embed: float32 [256], replicated, may hold values from -3 to 3
- conv_weight: bfloat16 [9, 256, 256], replicated, may hold values from -0.125 to 0.125
- norm_gain: float32 [256], replicated, may hold values from 0.5 to 1.5
- query_weight: bfloat16 [256, 256], replicated, may hold values from -0.375 to 0.375
- memory_weight: bfloat16 [512, 256], replicated, may hold values from -0.375 to 0.375
- attend_out: bfloat16 [256, 256], replicated, may hold values from -0.375 to 0.375
- decode_weight: bfloat16 [69, 256], replicated, may hold values from -0.375 to 0.375
Outputs:
- queue_after: float32 [32, 69, 4, 256], P('noise', None, 'tile')
Inputs may be any that keep to these rules, and one draw needn't show every extreme that they name: The tiles fill a grid of 2 rows and 2 columns, each tile once, in an arrangement drawn per run; west and east neighbours run along a row, which closes into a loop; -1 stands for the missing north neighbour of the first row and south neighbour of the last row.
All inputs are finite; a program needn't handle non-finite values.
Results may differ from a plain program's by a relative error of at most 0.012.
Values may be sent and summed in bfloat16 or wider, within the bound.
A program may use at most 64 MiB of HBM per device.

v0:
```python
import functools
import math

import jax
import jax.numpy as jnp
from jax import lax
from jax.experimental import pallas as pl
from jax.experimental.pallas import tpu as pltpu
from jax.sharding import PartitionSpec as P

HEADS = 8
MESH = pl.DeviceIdType.MESH
BF = jnp.bfloat16
F32 = jnp.float32


def dot_t(left, right):
    return lax.dot_general(left, right, (((1,), (1,)), ((), ())), preferred_element_type=F32)


def dot_n(left, right):
    return lax.dot_general(left, right, (((1,), (0,)), ((), ())), preferred_element_type=F32)


def kernel(
    groups, tiles, levels, plan, neighbours, queue, noise, in_weight, level_embed, conv_weight,
    norm_gain, query_weight, memory_weight, attend_out, decode_weight, out,
    frames_f32, own_low, next_low, second_low, own_edges, own_edges_1, next_edges, next_edges_1,
    second_edges, second_edges_1, noise_edges,
    sigma_own, sigma_next, lift_weight, head_sum, head_spread, pick, scaled, halo, halo_lifted,
    padded, hidden, normed, queries, memory, scores,
    send_sems, own_sems, next_sems, second_sems, noise_sems, frame_sems,
):
    frame_count, fields, cells = queue.shape
    steps = noise.shape[0]
    width = in_weight.shape[0]
    side = math.isqrt(cells)
    head_size = width // HEADS
    reach = 2 * frame_count
    own_edges = (own_edges, own_edges_1)
    next_edges = (next_edges, next_edges_1)
    second_edges = (second_edges, second_edges_1)
    me = lax.axis_index("tile")
    group = lax.axis_index("noise")
    is_last = group == groups - 1
    is_tail = group == groups - 2

    def tile_at(k):
        return lax.rem(me + k, tiles)

    barrier = pltpu.get_barrier_semaphore()
    for k in range(1, tiles):
        pl.semaphore_signal(
            barrier, 1, device_id={"noise": group, "tile": tile_at(k)}, device_id_type=MESH
        )
    for away in (-2, -1, 1, 2):
        @pl.when(jnp.logical_and(group + away >= 0, group + away < groups))
        def _():
            for k in range(tiles):
                pl.semaphore_signal(
                    barrier, 1, device_id={"noise": group + away, "tile": tile_at(k)},
                    device_id_type=MESH,
                )

    row = lax.broadcasted_iota(jnp.int32, (cells, 128), 0)
    lane = lax.broadcasted_iota(jnp.int32, (cells, 128), 1)
    part = lane % 64 // side
    spot = lane % side
    target = jnp.where(
        part == 0, spot, jnp.where(part == 1, (side - 1) * side + spot, jnp.where(
            part == 2, spot * side, spot * side + side - 1)))
    hit = row == target
    pick[0] = jnp.where(jnp.logical_and(hit, lane < 64), 1.0, 0.0).astype(BF)
    pick[1] = jnp.where(jnp.logical_and(hit, lane >= 64), 1.0, 0.0).astype(BF)
    channel = lax.broadcasted_iota(jnp.int32, (frame_count * width, 128), 0)
    head_lane = lax.broadcasted_iota(jnp.int32, (frame_count * width, 128), 1)
    head_sum[...] = jnp.where(channel // head_size == head_lane, 1.0, 0.0).astype(BF)
    channel = lax.broadcasted_iota(jnp.int32, (128, frame_count * width), 1)
    head_lane = lax.broadcasted_iota(jnp.int32, (128, frame_count * width), 0)
    head_spread[...] = jnp.where(channel // head_size == head_lane, 1.0, 0.0).astype(BF)
    lift_weight[...] = jnp.zeros_like(lift_weight)
    lift_weight[:, :fields] = in_weight[...]
    scaled[...] = jnp.zeros_like(scaled)
    halo[...] = jnp.zeros_like(halo)
    sigma_own[...] = jnp.ones_like(sigma_own)
    deltas = []
    for i in range(frame_count):
        sigma_own[i : i + 1] = jnp.full((1, 256), plan[levels[i]], F32)
        deltas.append(jnp.full((1, 256), plan[levels[i] + 1], F32))

    @pl.when(is_last)
    def _():
        sigma_next[...] = jnp.ones_like(sigma_next)
        next_low[...] = jnp.zeros_like(next_low)
        for edges in next_edges:
            edges[...] = jnp.zeros_like(edges)

    @pl.when(group >= groups - 2)
    def _():
        second_low[...] = jnp.zeros_like(second_low)
        for edges in second_edges:
            edges[...] = jnp.zeros_like(edges)

    frames_f32[:frame_count] = queue[...]
    for s in range(steps):
        both = dot_n(noise[s].astype(BF), pick[0] + pick[1])
        noise_edges[me, s] = both.astype(BF)

    west, east = neighbours[me, 0], neighbours[me, 1]
    north, south = neighbours[me, 2], neighbours[me, 3]
    north_in, south_in = jnp.maximum(north, 0), jnp.maximum(south, 0)
    north_west, north_east = neighbours[north_in, 0], neighbours[north_in, 1]
    south_west, south_east = neighbours[south_in, 0], neighbours[south_in, 1]
    around = [jnp.maximum(t, 0) for t in (south, north, east, west)]
    corner = [jnp.maximum(t, 0) for t in (south_east, south_west, north_east, north_west)]

    def copy(source, target_ref, send, recv, where):
        return pltpu.make_async_remote_copy(
            src_ref=source, dst_ref=target_ref, send_sem=send, recv_sem=recv,
            device_id=where, device_id_type=MESH,
        )

    def to_own(step, k, sender):
        return copy(
            own_edges[step].at[sender], own_edges[step].at[sender], send_sems.at[step, 0, k],
            own_sems.at[step, sender], {"noise": group, "tile": tile_at(k)},
        )

    def to_noise(k, sender):
        return copy(
            noise_edges.at[sender], noise_edges.at[sender], send_sems.at[0, 3, k],
            noise_sems.at[sender], {"noise": group, "tile": tile_at(k)},
        )

    def to_next(step, k, sender):
        return copy(
            own_edges[step].at[sender], next_edges[step].at[sender], send_sems.at[step, 1, k],
            next_sems.at[step, sender], {"noise": group - 1, "tile": tile_at(k)},
        )

    def to_second(step, k, sender):
        return copy(
            own_edges[step].at[sender, 0], second_edges[step].at[sender], send_sems.at[step, 2, k],
            second_sems.at[step, sender], {"noise": group - 2, "tile": tile_at(k)},
        )

    def frame_copy(step):
        return copy(
            own_low.at[step], next_low.at[step], send_sems.at[step, 4, 0], frame_sems.at[step, 0],
            {"noise": group - 1, "tile": me},
        )

    def front_copy(step):
        return copy(
            own_low.at[step, 0], second_low.at[step], send_sems.at[step, 4, 1],
            frame_sems.at[step, 1], {"noise": group - 2, "tile": me},
        )

    def sigma_copy():
        return copy(
            sigma_own, sigma_next, send_sems.at[0, 4, 2], frame_sems.at[0, 2],
            {"noise": group - 1, "tile": me},
        )

    def prepare(step):
        for f in range(frame_count):
            own_low[step, f] = frames_f32[f].astype(BF)
        for pair in range(frame_count // 2):
            edges = dot_n(own_low[step, 2 * pair], pick[0]) + dot_n(
                own_low[step, 2 * pair + 1], pick[1]
            )
            own_edges[step][me, pair] = edges.astype(BF)

    def send(step, first):
        for k in range(1, tiles):
            to_own(step, k, me).start()
            if first:
                to_noise(k, me).start()

        @pl.when(group >= 1)
        def _():
            if first:
                sigma_copy().start()
            frame_copy(step).start()
            for k in range(tiles):
                to_next(step, k, me).start()

        @pl.when(group >= 2)
        def _():
            front_copy(step).start()
            for k in range(tiles):
                to_second(step, k, me).start()

    def arrive(step, first):
        for k in range(1, tiles):
            to_own(step, k, tile_at(k)).wait_recv()
            if first:
                to_noise(k, tile_at(k)).wait_recv()

        @pl.when(group < groups - 1)
        def _():
            if first:
                sigma_copy().wait_recv()
            frame_copy(step).wait_recv()
            for k in range(tiles):
                to_next(step, k, tile_at(k)).wait_recv()

        @pl.when(group < groups - 2)
        def _():
            front_copy(step).wait_recv()
            for k in range(tiles):
                to_second(step, k, tile_at(k)).wait_recv()

    def sent(step, first):
        for k in range(1, tiles):
            to_own(step, k, me).wait_send()
            if first:
                to_noise(k, me).wait_send()

        @pl.when(group >= 1)
        def _():
            if first:
                sigma_copy().wait_send()
            frame_copy(step).wait_send()
            for k in range(tiles):
                to_next(step, k, me).wait_send()

        @pl.when(group >= 2)
        def _():
            front_copy(step).wait_send()
            for k in range(tiles):
                to_second(step, k, me).wait_send()

    def sigma_of(position):
        if position < frame_count:
            return sigma_own[position : position + 1]
        return sigma_next[position - frame_count : position - frame_count + 1]

    lane1 = lax.broadcasted_iota(jnp.int32, (1, 128), 1)
    slot = lane1 % 64 // side

    def halo_of(step, pair):
        if pair < frame_count // 2:
            load = lambda t: own_edges[step][t, pair].astype(F32)
        elif pair < frame_count:
            load = lambda t: next_edges[step][t, pair - frame_count // 2].astype(F32)
        else:
            load = lambda t: second_edges[step][t].astype(F32)
        fresh = None
        if pair == frame_count // 2:
            take, scale = jnp.logical_and(is_last, lane1 < 64), sigma_own
            fresh = True
        elif pair == frame_count:
            take, scale = jnp.logical_and(is_tail, lane1 < 64), sigma_next
            fresh = True

        def load_all(t):
            value = load(t)
            if fresh:
                fresh_value = noise_edges[t, step].astype(F32) * scale[
                    frame_count - 1 : frame_count, :128
                ]
                value = jnp.where(take, fresh_value, value)
            return value

        parts = [load_all(t) for t in around]
        middle = jnp.where(slot == 0, parts[0], jnp.where(
            slot == 1, parts[1], jnp.where(slot == 2, parts[2], parts[3])))
        parts = [load_all(t) for t in corner]
        place = lane1 % 64
        ends = jnp.where(place == 0, parts[0], jnp.where(
            place == side - 1, parts[1], jnp.where(place == side, parts[2], parts[3])))
        low = sigma_of(max(2 * pair - 1, 0))
        high = sigma_of(min(2 * pair, reach - 1))
        sigma = jnp.where(lane1 < 64, low[:, :128], high[:, :128])
        in_scale = lax.rsqrt(sigma * sigma + 1.0)
        halo[pair, :fields, :128] = middle * in_scale
        halo[pair, :fields, 128:] = ends * in_scale
        turned = halo[pair].T.astype(BF)
        rows = lax.broadcasted_iota(jnp.int32, (256, 1), 0) % 128
        bias = jnp.where(rows < 64, jnp.log(low), jnp.log(high)) * level_embed[...]
        lifted = dot_t(turned, lift_weight[...]) + bias
        kind = rows % 64 // side
        there = jnp.where(kind == 0, south, jnp.where(kind == 1, north, jnp.where(
            kind == 2, east, west)))
        lifted = jnp.where(there >= 0, lifted, 0.0)
        halo_lifted[pair] = lifted.astype(BF).astype(F32)

    def lift(step, position):
        sigma = sigma_of(position)
        in_scale = lax.rsqrt(sigma * sigma + 1.0)
        frame = position + 1
        if frame < frame_count:
            value = frames_f32[frame]
        elif frame < reach:
            value = next_low[step, frame - frame_count].astype(F32)
            if frame == frame_count:
                entering = sigma_own[frame_count - 1 : frame_count] * noise[step]
                value = jnp.where(is_last, entering, value)
                frames_f32[frame] = value
        else:
            value = second_low[step].astype(F32)
            entering = sigma_next[frame_count - 1 : frame_count] * noise[step]
            value = jnp.where(is_tail, entering, value)
        scaled[position % 2, :fields] = value * in_scale
        turned = scaled[position % 2].T.astype(BF)
        lifted = dot_t(turned, lift_weight[...]) + jnp.log(sigma) * level_embed[...]
        lifted = lifted.astype(BF).astype(F32)
        pair, base = frame // 2, frame % 2 * 64
        south_row = halo_lifted[pair, base : base + side]
        north_row = halo_lifted[pair, base + side : base + 2 * side]
        tall = jnp.concatenate([north_row, lifted, south_row], axis=0)
        padded[position, :, width : 2 * width] = tall.astype(BF)
        east_col, west_col = base + 2 * side, base + 3 * side
        ends = 128 + base
        west_rows = [ends + 2 * side - 1] + [west_col + y for y in range(side)] + [ends + side - 1]
        east_rows = [ends + side] + [east_col + y for y in range(side)] + [ends]

        def spread(rows):
            return jnp.concatenate([
                jnp.broadcast_to(halo_lifted[pair, r : r + 1], (side, width)) for r in rows
            ], axis=0)

        total = (side + 2) * side
        along = lax.broadcasted_iota(jnp.int32, (total, 1), 0) % side
        from_west = jnp.where(along == 0, spread(west_rows), pltpu.roll(tall, 1, 0))
        padded[position, :, :width] = from_west.astype(BF)
        from_east = jnp.where(along == side - 1, spread(east_rows), pltpu.roll(tall, total - 1, 0))
        padded[position, :, 2 * width :] = from_east.astype(BF)

    def convolve(index):
        total = None
        for offset in range(9):
            down, right = offset // 3, offset % 3
            window = padded[index, down * side : down * side + cells, right * width : (right + 1) * width]
            product = dot_t(window, conv_weight[offset])
            total = product if total is None else total + product
        centre = padded[index, side : side + cells, width : 2 * width].astype(F32)
        result = (centre + total / (1.0 + jnp.exp(-total))).astype(BF)
        hidden[index] = result
        widened = result.astype(F32)
        mean = jnp.mean(widened * widened, axis=1, keepdims=True)
        norm = (widened * lax.rsqrt(mean + 1e-06) * norm_gain[...]).astype(BF)
        memory[index] = dot_t(norm, memory_weight[...]).astype(BF)
        normed[index] = norm

    rows_at_once = 128

    def attend(chunk):
        begin = pl.multiple_of(chunk * rows_at_once, rows_at_once)
        here = pl.ds(begin, rows_at_once)
        most = None
        for j in range(reach):
            keys = memory[j, here, :width]
            products = jnp.concatenate([queries[i, here] * keys for i in range(frame_count)], axis=1)
            score = dot_n(products, head_sum[...]) * head_size ** (-0.5)
            if j >= frame_count:
                score = jnp.where(is_last, -jnp.inf, score)
            scores[j] = score
            most = score if most is None else jnp.maximum(most, score)
        total = None
        for j in range(reach):
            raised = jnp.exp(scores[j] - most)
            scores[j] = raised
            total = raised if total is None else total + raised
        inverse = 1.0 / total
        context = [None] * frame_count
        for j in range(reach):
            weight = (scores[j] * inverse).astype(BF)
            values = memory[j, here, width:].astype(F32)
            for i in range(frame_count):
                spread = dot_n(weight, head_spread[:, i * width : (i + 1) * width]) * values
                context[i] = spread if context[i] is None else context[i] + spread
        for i in range(frame_count):
            refined = hidden[i, here].astype(F32) + dot_t(context[i].astype(BF), attend_out[...])
            projected = dot_t(decode_weight[...], refined.astype(BF))
            sigma = sigma_own[i : i + 1, :rows_at_once]
            spread = sigma * sigma + 1.0
            frame = frames_f32[i + 1, :, here]
            denoised = (1.0 / spread) * frame + (sigma * lax.rsqrt(spread)) * projected
            change = (deltas[i][:, :rows_at_once] - sigma) / sigma
            frames_f32[i, :, here] = frame + change * (frame - denoised)

    for step in range(steps):
        prepare(step)
        if step == 0:
            reached = sum(
                jnp.where(jnp.logical_and(group + away >= 0, group + away < groups), tiles, 0)
                for away in (-2, -1, 1, 2)
            )
            pl.semaphore_wait(barrier, tiles - 1 + reached)
        send(step, step == 0)
        arrive(step, step == 0)
        for pair in range(frame_count + 1):
            halo_of(step, pair)
        for position in range(reach):
            lift(step, position)
        lax.fori_loop(0, reach, lambda index, c: (convolve(index), c)[1], 0)
        for i in range(frame_count):
            queries[i] = dot_t(normed[i], query_weight[...]).astype(BF)
        lax.fori_loop(0, cells // rows_at_once, lambda chunk, c: (attend(chunk), c)[1], 0)
        sent(step, step == 0)
    out[...] = frames_f32[:frame_count]


def shards(groups, tiles, queue_state, fresh_noise, plan, levels, neighbours, in_weight, level_embed,
           conv_weight, norm_gain, query_weight, memory_weight, attend_out, decode_weight):
    frames, fields, _, cells = queue_state.shape
    steps = fresh_noise.shape[0]
    width = in_weight.shape[0]
    side = math.isqrt(cells)
    reach = 2 * frames
    vmem = pl.BlockSpec(memory_space=pltpu.VMEM)
    smem = pl.BlockSpec(memory_space=pltpu.SMEM)
    dma = pltpu.SemaphoreType.DMA
    result = pl.pallas_call(
        functools.partial(kernel, groups, tiles),
        out_shape=jax.ShapeDtypeStruct((frames, fields, cells), F32),
        in_specs=[smem] * 3 + [vmem] * 10,
        out_specs=vmem,
        scratch_shapes=[
            pltpu.VMEM((frames + 1, fields, cells), F32),
            pltpu.VMEM((steps, frames, fields, cells), BF),
            pltpu.VMEM((steps, frames, fields, cells), BF),
            pltpu.VMEM((steps, fields, cells), BF),
            pltpu.VMEM((tiles, frames // 2, fields, 128), BF),
            pltpu.VMEM((tiles, frames // 2, fields, 128), BF),
            pltpu.VMEM((tiles, frames // 2, fields, 128), BF),
            pltpu.VMEM((tiles, frames // 2, fields, 128), BF),
            pltpu.VMEM((tiles, fields, 128), BF),
            pltpu.VMEM((tiles, fields, 128), BF),
            pltpu.VMEM((tiles, steps, fields, 128), BF),
            pltpu.VMEM((8, 256), F32),
            pltpu.VMEM((8, 256), F32),
            pltpu.VMEM((width, 128), BF),
            pltpu.VMEM((frames * width, 128), BF),
            pltpu.VMEM((128, frames * width), BF),
            pltpu.VMEM((2, cells, 128), BF),
            pltpu.VMEM((2, 128, cells), F32),
            pltpu.VMEM((frames + 1, 128, 256), F32),
            pltpu.VMEM((frames + 1, 256, width), F32),
            pltpu.VMEM((reach, (side + 2) * side, 3 * width), BF),
            pltpu.VMEM((reach, cells, width), BF),
            pltpu.VMEM((reach, cells, width), BF),
            pltpu.VMEM((frames, cells, width), BF),
            pltpu.VMEM((reach, cells, 2 * width), BF),
            pltpu.VMEM((reach, 128, 128), F32),
            dma((steps, 5, max(tiles, 3))),
            dma((steps, tiles)),
            dma((steps, tiles)),
            dma((steps, tiles)),
            dma((tiles,)),
            dma((steps, 3)),
        ],
        compiler_params=pltpu.CompilerParams(
            collective_id=0, has_side_effects=True, vmem_limit_bytes=56 * 1024 * 1024
        ),
    )(
        levels, plan, neighbours, queue_state.reshape(frames, fields, cells),
        fresh_noise.reshape(steps, fields, cells), in_weight, level_embed.reshape(1, width),
        conv_weight, norm_gain.reshape(1, width), query_weight, memory_weight, attend_out,
        decode_weight,
    )
    return result.reshape(queue_state.shape)


def solution(mesh):
    body = functools.partial(shards, mesh.shape["noise"], mesh.shape["tile"])
    in_specs = (
        P("noise", None, "tile", None), P(None, None, "tile", None), P(), P("noise"),
    ) + (P(),) * 9
    return jax.shard_map(
        body, mesh=mesh, in_specs=in_specs, out_specs=P("noise", None, "tile", None), check_vma=False
    )
```

profile of v0, /device:TPU:0, one launch (start us, length us, event | category | flops | bytes accessed | tf_op | source)
XLA Modules:
  0.0 64.4 jit_solution(2711212028119408340)
XLA Ops:
  0.0 1.5 %copy.16.in_weight = bf16[256,69]{1,0:T(8,128)(2,1)} copy(bf16[256,69]{0,1:T(8,128)(2,1)} %param.18) | data formatting | bytes 70656 | tf_op args[5]
  1.5 1.6 %copy.23 = f32[2,69,1,256]{3,1,2,0:T(8,128)} copy(f32[2,69,1,256]{3,2,1,0:T(1,128)} %param.14) | data formatting | bytes 282624
  3.1 1.7 %copy.22 = f32[4,69,1,256]{3,1,2,0:T(8,128)} copy(f32[4,69,1,256]{3,2,1,0:T(1,128)} %param.13) | data formatting | bytes 565248
  4.8 57.7 %shard_map.127 = f32[4,69,256]{2,1,0:T(8,128)} custom-call(s32[4]{0:T(128)} %levels.1, f32[17]{0:T(128)} %plan.1, s32[4,4]{1,0:T(4,128)} %neighbours.1, f32[4,69,256]{2,1,0:T(8,128)} %bitcast.10, f32[2,69,256]{2,1,0:T(8,128)} %bitcast.11, bf16[256,69]{1,0:T(8,128)(2,1)} %copy.16.in_weight, f32[1,256]{1,0:T(1,128)} %bitcast.12, ...), custom_call_target="tpu_custom_call" | custom-call | tf_op jit(solution)/shard_map/pallas_call | solution.py:416
  62.5 2.0 %copy.17 = f32[4,69,1,256]{3,2,1,0:T(1,128)} copy(f32[4,69,1,256]{3,1,0,2:T(8,128)} %bitcast.9) | data formatting | bytes 565248 | tf_op jit(solution)/shard_map/reshape | solution.py:464
where the time goes:
time: 64.7 us; the launch traced here: 64.4 us
  Pallas kernels  57.7 us (89%)
  local copies, waits for them, and re-layouts  6.72 us (10%)
    pallas_call x1, Pallas kernels, shards(): pl.pallas_call(functools.partial(kernel, groups, tiles), out_shape=jax.Sh...  57.7 us
    unnamed x3, local copies, waits for them, and re-layouts  4.76 us
    reshape x1, local copies, waits for them, and re-layouts, shards(): return result.reshape(queue_state.shape)  1.96 us

commit v1 on v0

--- a/solution.py
+++ b/solution.py
@@ -23,17 +23,18 @@
 
 
 def kernel(
-    groups, tiles, levels, plan, neighbours, queue, noise, in_weight, level_embed, conv_weight,
-    norm_gain, query_weight, memory_weight, attend_out, decode_weight, out,
-    frames_f32, own_low, next_low, second_low, own_edges, own_edges_1, next_edges, next_edges_1,
+    groups, tiles, levels, plan, neighbours, queue, noise_rows, in_weight, level_embed, conv_hbm,
+    norm_gain, query_raw, memory_raw, attend_raw, decode_weight, out,
+    conv_weight, query_weight, memory_weight, attend_out, noise, frames_f32, own_low, next_low, second_low, own_edges, own_edges_1, next_edges, next_edges_1,
     second_edges, second_edges_1, noise_edges,
     sigma_own, sigma_next, lift_weight, head_sum, head_spread, pick, scaled, halo, halo_lifted,
-    padded, hidden, normed, queries, memory, scores,
+    padded, hidden, normed, queries, memory, load_sem,
     send_sems, own_sems, next_sems, second_sems, noise_sems, frame_sems,
 ):
-    frame_count, fields, cells = queue.shape
-    steps = noise.shape[0]
-    width = in_weight.shape[0]
+    frame_count, fields, cells = padded.shape[0] // 2, in_weight.shape[0], hidden.shape[1]
+    steps = own_low.shape[0]
+    width = in_weight.shape[1]
+    halves = cells // 128
     side = math.isqrt(cells)
     head_size = width // HEADS
     reach = 2 * frame_count
@@ -48,6 +49,8 @@
     def tile_at(k):
         return lax.rem(me + k, tiles)
 
+    load = pltpu.make_async_copy(conv_hbm, conv_weight, load_sem)
+    load.start()
     barrier = pltpu.get_barrier_semaphore()
     for k in range(1, tiles):
         pl.semaphore_signal(
@@ -72,14 +75,24 @@
     hit = row == target
     pick[0] = jnp.where(jnp.logical_and(hit, lane < 64), 1.0, 0.0).astype(BF)
     pick[1] = jnp.where(jnp.logical_and(hit, lane >= 64), 1.0, 0.0).astype(BF)
-    channel = lax.broadcasted_iota(jnp.int32, (frame_count * width, 128), 0)
-    head_lane = lax.broadcasted_iota(jnp.int32, (frame_count * width, 128), 1)
-    head_sum[...] = jnp.where(channel // head_size == head_lane, 1.0, 0.0).astype(BF)
-    channel = lax.broadcasted_iota(jnp.int32, (128, frame_count * width), 1)
-    head_lane = lax.broadcasted_iota(jnp.int32, (128, frame_count * width), 0)
-    head_spread[...] = jnp.where(channel // head_size == head_lane, 1.0, 0.0).astype(BF)
+    pairs = frame_count * frame_count
+    source = lax.broadcasted_iota(jnp.int32, (pairs // 2 * 128, 128), 0)
+    target = lax.broadcasted_iota(jnp.int32, (pairs // 2 * 128, 128), 1)
+    low = source % 128
+    combo = source // 128 + jnp.where(low >= 64, pairs // 2, 0)
+    head_sum[...] = jnp.where(target == combo * HEADS + low % HEADS, 1.0, 0.0).astype(BF)
+    source = lax.broadcasted_iota(jnp.int32, (128, pairs * 128), 0)
+    target = lax.broadcasted_iota(jnp.int32, (128, pairs * 128), 1)
+    place = target // 128
+    combo = place % frame_count * frame_count + place // frame_count
+    head_spread[...] = jnp.where(source == combo * HEADS + target % HEADS, 1.0, 0.0).astype(BF)
+    source = lax.broadcasted_iota(jnp.int32, (width, width), 1)
+    target = lax.broadcasted_iota(jnp.int32, (width, width), 0)
+    order = jnp.where(
+        source == target % HEADS * head_size + target // HEADS, 1.0, 0.0
+    ).astype(BF)
     lift_weight[...] = jnp.zeros_like(lift_weight)
-    lift_weight[:, :fields] = in_weight[...]
+    lift_weight[:fields] = in_weight[...]
     scaled[...] = jnp.zeros_like(scaled)
     halo[...] = jnp.zeros_like(halo)
     sigma_own[...] = jnp.ones_like(sigma_own)
@@ -101,7 +114,12 @@
         for edges in second_edges:
             edges[...] = jnp.zeros_like(edges)
 
-    frames_f32[:frame_count] = queue[...]
+    for half in range(halves):
+        across = slice(half * 128, (half + 1) * 128)
+        for i in range(frame_count):
+            frames_f32[i, :, across] = queue[pl.ds(i * halves * fields + half, fields, halves), :]
+        for i in range(steps):
+            noise[i, :, across] = noise_rows[pl.ds(i * halves * fields + half, fields, halves), :]
     for s in range(steps):
         both = dot_n(noise[s].astype(BF), pick[0] + pick[1])
         noise_edges[me, s] = both.astype(BF)
@@ -182,33 +200,35 @@
             if first:
                 sigma_copy().start()
             frame_copy(step).start()
-            for k in range(tiles):
+            for k in range(1, tiles):
                 to_next(step, k, me).start()
 
         @pl.when(group >= 2)
         def _():
             front_copy(step).start()
-            for k in range(tiles):
+            for k in range(1, tiles):
                 to_second(step, k, me).start()
 
-    def arrive(step, first):
+    def arrive_own(step, first):
         for k in range(1, tiles):
             to_own(step, k, tile_at(k)).wait_recv()
             if first:
                 to_noise(k, tile_at(k)).wait_recv()
 
+    def arrive_next(step, first):
         @pl.when(group < groups - 1)
         def _():
             if first:
                 sigma_copy().wait_recv()
             frame_copy(step).wait_recv()
-            for k in range(tiles):
+            for k in range(1, tiles):
                 to_next(step, k, tile_at(k)).wait_recv()
 
+    def arrive_second(step):
         @pl.when(group < groups - 2)
         def _():
             front_copy(step).wait_recv()
-            for k in range(tiles):
+            for k in range(1, tiles):
                 to_second(step, k, tile_at(k)).wait_recv()
 
     def sent(step, first):
@@ -222,13 +242,13 @@
             if first:
                 sigma_copy().wait_send()
             frame_copy(step).wait_send()
-            for k in range(tiles):
+            for k in range(1, tiles):
                 to_next(step, k, me).wait_send()
 
         @pl.when(group >= 2)
         def _():
             front_copy(step).wait_send()
-            for k in range(tiles):
+            for k in range(1, tiles):
                 to_second(step, k, me).wait_send()
 
     def sigma_of(position):
@@ -279,7 +299,7 @@
         turned = halo[pair].T.astype(BF)
         rows = lax.broadcasted_iota(jnp.int32, (256, 1), 0) % 128
         bias = jnp.where(rows < 64, jnp.log(low), jnp.log(high)) * level_embed[...]
-        lifted = dot_t(turned, lift_weight[...]) + bias
+        lifted = dot_n(turned, lift_weight[...]) + bias
         kind = rows % 64 // side
         there = jnp.where(kind == 0, south, jnp.where(kind == 1, north, jnp.where(
             kind == 2, east, west)))
@@ -304,7 +324,7 @@
             value = jnp.where(is_tail, entering, value)
         scaled[position % 2, :fields] = value * in_scale
         turned = scaled[position % 2].T.astype(BF)
-        lifted = dot_t(turned, lift_weight[...]) + jnp.log(sigma) * level_embed[...]
+        lifted = dot_n(turned, lift_weight[...]) + jnp.log(sigma) * level_embed[...]
         lifted = lifted.astype(BF).astype(F32)
         pair, base = frame // 2, frame % 2 * 64
         south_row = halo_lifted[pair, base : base + side]
@@ -349,30 +369,50 @@
     def attend(chunk):
         begin = pl.multiple_of(chunk * rows_at_once, rows_at_once)
         here = pl.ds(begin, rows_at_once)
-        most = None
-        for j in range(reach):
-            keys = memory[j, here, :width]
-            products = jnp.concatenate([queries[i, here] * keys for i in range(frame_count)], axis=1)
-            score = dot_n(products, head_sum[...]) * head_size ** (-0.5)
-            if j >= frame_count:
-                score = jnp.where(is_last, -jnp.inf, score)
-            scores[j] = score
-            most = score if most is None else jnp.maximum(most, score)
-        total = None
-        for j in range(reach):
-            raised = jnp.exp(scores[j] - most)
-            scores[j] = raised
-            total = raised if total is None else total + raised
+        lower = lax.broadcasted_iota(jnp.int32, (1, 128), 1) < 64
+        asked = [queries[i, here].astype(F32) for i in range(frame_count)]
+
+        def partial(i, j):
+            product = asked[i] * memory[j, here, :width].astype(F32)
+            total = product[:, :128]
+            for start in range(128, width, 128):
+                total = total + product[:, start : start + 128]
+            return total
+
+        def score_block(first):
+            pieces = []
+            for c in range(pairs // 2):
+                later = c + pairs // 2
+                one = partial(c % frame_count, first + c // frame_count)
+                two = partial(later % frame_count, first + later // frame_count)
+                swapped = pltpu.roll(jnp.where(lower, two, one), 64, 1)
+                pieces.append((jnp.where(lower, one, two) + swapped).astype(BF))
+            return dot_n(jnp.concatenate(pieces, axis=1), head_sum[...]) * head_size ** (-0.5)
+
+        near = score_block(0)
+        far = jnp.where(is_last, -jnp.inf, score_block(frame_count))
+        most = jnp.maximum(near, far)
+        most = jnp.maximum(most, pltpu.roll(most, 64, 1))
+        most = jnp.maximum(most, pltpu.roll(most, 32, 1))
+        near = jnp.exp(near - most)
+        far = jnp.exp(far - most)
+        total = near + far
+        total = total + pltpu.roll(total, 64, 1)
+        total = total + pltpu.roll(total, 32, 1)
         inverse = 1.0 / total
-        context = [None] * frame_count
-        for j in range(reach):
-            weight = (scores[j] * inverse).astype(BF)
-            values = memory[j, here, width:].astype(F32)
-            for i in range(frame_count):
-                spread = dot_n(weight, head_spread[:, i * width : (i + 1) * width]) * values
-                context[i] = spread if context[i] is None else context[i] + spread
+        near = (near * inverse).astype(BF)
+        far = (far * inverse).astype(BF)
         for i in range(frame_count):
-            refined = hidden[i, here].astype(F32) + dot_t(context[i].astype(BF), attend_out[...])
+            context = None
+            columns = slice(i * frame_count * 128, (i + 1) * frame_count * 128)
+            for block, weight in enumerate((near, far)):
+                spread = dot_n(weight, head_spread[:, columns])
+                for at in range(frame_count):
+                    wide = spread[:, at * 128 : (at + 1) * 128]
+                    values = memory[block * frame_count + at, here, width:].astype(F32)
+                    term = jnp.concatenate([wide] * (width // 128), axis=1) * values
+                    context = term if context is None else context + term
+            refined = hidden[i, here].astype(F32) + dot_t(context.astype(BF), attend_out[...])
             projected = dot_t(decode_weight[...], refined.astype(BF))
             sigma = sigma_own[i : i + 1, :rows_at_once]
             spread = sigma * sigma + 1.0
@@ -390,17 +430,37 @@
             )
             pl.semaphore_wait(barrier, tiles - 1 + reached)
         send(step, step == 0)
-        arrive(step, step == 0)
-        for pair in range(frame_count + 1):
+        if step == 0:
+            query_weight[...] = dot_n(order, query_raw[...]).astype(BF)
+            memory_weight[:width] = dot_n(order, memory_raw[:width]).astype(BF)
+            memory_weight[width:] = dot_n(order, memory_raw[width:]).astype(BF)
+            attend_out[...] = dot_t(attend_raw[...], order).astype(BF)
+        half = frame_count // 2
+        arrive_own(step, step == 0)
+        for pair in range(half):
             halo_of(step, pair)
-        for position in range(reach):
+        for position in range(frame_count - 1):
             lift(step, position)
-        lax.fori_loop(0, reach, lambda index, c: (convolve(index), c)[1], 0)
+        if step == 0:
+            load.wait()
+        lax.fori_loop(0, frame_count - 1, lambda index, c: (convolve(index), c)[1], 0)
+        arrive_next(step, step == 0)
+        for pair in range(half, frame_count):
+            halo_of(step, pair)
+        for position in range(frame_count - 1, reach - 1):
+            lift(step, position)
+        arrive_second(step)
+        halo_of(step, frame_count)
+        lift(step, reach - 1)
+        lax.fori_loop(frame_count - 1, reach, lambda index, c: (convolve(index), c)[1], 0)
         for i in range(frame_count):
             queries[i] = dot_t(normed[i], query_weight[...]).astype(BF)
         lax.fori_loop(0, cells // rows_at_once, lambda chunk, c: (attend(chunk), c)[1], 0)
         sent(step, step == 0)
-    out[...] = frames_f32[:frame_count]
+    for half in range(halves):
+        across = slice(half * 128, (half + 1) * 128)
+        for i in range(frame_count):
+            out[pl.ds(i * halves * fields + half, fields, halves), :] = frames_f32[i, :, across]
 
 
 def shards(groups, tiles, queue_state, fresh_noise, plan, levels, neighbours, in_weight, level_embed,
@@ -415,10 +475,15 @@
     dma = pltpu.SemaphoreType.DMA
     result = pl.pallas_call(
         functools.partial(kernel, groups, tiles),
-        out_shape=jax.ShapeDtypeStruct((frames, fields, cells), F32),
-        in_specs=[smem] * 3 + [vmem] * 10,
+        out_shape=jax.ShapeDtypeStruct((frames * fields * cells // 128, 128), F32),
+        in_specs=[smem] * 3 + [vmem] * 4 + [pl.BlockSpec(memory_space=pl.ANY)] + [vmem] * 5,
         out_specs=vmem,
         scratch_shapes=[
+            pltpu.VMEM(conv_weight.shape, BF),
+            pltpu.VMEM(query_weight.shape, BF),
+            pltpu.VMEM(memory_weight.shape, BF),
+            pltpu.VMEM(attend_out.shape, BF),
+            pltpu.VMEM((steps, fields, cells), F32),
             pltpu.VMEM((frames + 1, fields, cells), F32),
             pltpu.VMEM((steps, frames, fields, cells), BF),
             pltpu.VMEM((steps, frames, fields, cells), BF),
@@ -432,9 +497,9 @@
             pltpu.VMEM((tiles, steps, fields, 128), BF),
             pltpu.VMEM((8, 256), F32),
             pltpu.VMEM((8, 256), F32),
-            pltpu.VMEM((width, 128), BF),
-            pltpu.VMEM((frames * width, 128), BF),
-            pltpu.VMEM((128, frames * width), BF),
+            pltpu.VMEM((128, width), BF),
+            pltpu.VMEM((frames * frames * 64, 128), BF),
+            pltpu.VMEM((128, frames * frames * 128), BF),
             pltpu.VMEM((2, cells, 128), BF),
             pltpu.VMEM((2, 128, cells), F32),
             pltpu.VMEM((frames + 1, 128, 256), F32),
@@ -444,7 +509,7 @@
             pltpu.VMEM((reach, cells, width), BF),
             pltpu.VMEM((frames, cells, width), BF),
             pltpu.VMEM((reach, cells, 2 * width), BF),
-            pltpu.VMEM((reach, 128, 128), F32),
+            dma,
             dma((steps, 5, max(tiles, 3))),
             dma((steps, tiles)),
             dma((steps, tiles)),
@@ -456,8 +521,8 @@
             collective_id=0, has_side_effects=True, vmem_limit_bytes=56 * 1024 * 1024
         ),
     )(
-        levels, plan, neighbours, queue_state.reshape(frames, fields, cells),
-        fresh_noise.reshape(steps, fields, cells), in_weight, level_embed.reshape(1, width),
+        levels, plan, neighbours, queue_state.reshape(-1, 128),
+        fresh_noise.reshape(-1, 128), in_weight.T, level_embed.reshape(1, width),
         conv_weight, norm_gain.reshape(1, width), query_weight, memory_weight, attend_out,
         decode_weight,
     )

time: 64.7 us -> 51.8 us (0.80)
  Pallas kernels: 57.7 us -> 47.8 us
  local copies, waits for them, and re-layouts: 6.72 us -> 2.53 us
  other arithmetic: 0 us -> 1.25 us
    pallas_call x1, Pallas kernels: 57.7 us -> 47.8 us  [shards(): pl.pallas_call(functools.partial(kernel, groups, tiles), out_shape=jax.Sh...]
    unnamed x3 -> x1, local copies, waits for them, and re-layouts: 4.76 us -> 1.86 us
    reshape x1, local copies, waits for them, and re-layouts: 1.96 us -> 0.67 us  [shards(): fresh_noise.reshape(-1, 128)]
    unnamed x0 -> x1, other arithmetic: none -> 1.25 us
where the time goes in v1:
time: 51.8 us; the launch traced here: 51.6 us
  Pallas kernels  47.8 us (92%)
  local copies, waits for them, and re-layouts  2.53 us (5%)
  other arithmetic  1.25 us (2%)
    pallas_call x1, Pallas kernels, shards(): pl.pallas_call(functools.partial(kernel, groups, tiles), out_shape=jax.Sh...  47.8 us
    unnamed x1, local copies, waits for them, and re-layouts  1.86 us
    unnamed x1, other arithmetic  1.25 us

profile of v1, /device:TPU:0, one launch (start us, length us, event | category | flops | bytes accessed | tf_op | source)
XLA Modules:
  0.0 51.6 jit_solution(2379096900275518547)
XLA Ops:
  0.0 1.2 %reduce = f32[2,69,256]{2,1,0:T(8,128)S(1)} reduce(f32[2,69,1,256]{3,2,1,0:T(1,128)} %param.14, f32[]{:T(128)} %constant.3), dimensions={2}, to_apply=%param.14.reduce_sub_computation | reduce | bytes 282628 | tf_op args[1]
  1.2 0.7 %reshape.16.noise_rows = f32[276,128]{1,0:T(8,128)} reshape(f32[2,69,256]{2,1,0:T(8,128)S(1)} %reduce) | data formatting | bytes 282624 | tf_op jit(solution)/shard_map/reshape | solution.py:525
  1.9 47.8 %shard_map.127 = f32[552,128]{1,0:T(8,128)} custom-call(s32[4]{0:T(128)} %levels.1, f32[17]{0:T(128)} %plan.1, s32[4,4]{1,0:T(4,128)} %neighbours.1, f32[552,128]{1,0:T(8,128)} %bitcast.6, f32[276,128]{1,0:T(8,128)} %reshape.16.noise_rows, bf16[69,256]{1,0:T(8,128)(2,1)} %bitcast.7, f32[1,256]{1,0:T(1,128)} %bitcast.8, bf16[9,256,256]{2,1,0:T(8,128)(2,1)} %conv_hbm.1, ...), custom_call_target="tpu_custom_call" | custom-call | tf_op jit(solution)/shard_map/pallas_call | solution.py:476
  49.7 1.9 %copy.17 = f32[4,69,1,256]{3,2,1,0:T(1,128)} copy(f32[4,69,1,256]{3,2,1,0:T(1,128)} %bitcast.5) | data formatting | bytes 565248

commit v2 on v1

--- a/solution.py
+++ b/solution.py
@@ -76,10 +76,10 @@
     pick[0] = jnp.where(jnp.logical_and(hit, lane < 64), 1.0, 0.0).astype(BF)
     pick[1] = jnp.where(jnp.logical_and(hit, lane >= 64), 1.0, 0.0).astype(BF)
     pairs = frame_count * frame_count
-    source = lax.broadcasted_iota(jnp.int32, (pairs // 2 * 128, 128), 0)
-    target = lax.broadcasted_iota(jnp.int32, (pairs // 2 * 128, 128), 1)
+    source = lax.broadcasted_iota(jnp.int32, (pairs * 128, 128), 0)
+    target = lax.broadcasted_iota(jnp.int32, (pairs * 128, 128), 1)
     low = source % 128
-    combo = source // 128 + jnp.where(low >= 64, pairs // 2, 0)
+    combo = source // 128
     head_sum[...] = jnp.where(target == combo * HEADS + low % HEADS, 1.0, 0.0).astype(BF)
     source = lax.broadcasted_iota(jnp.int32, (128, pairs * 128), 0)
     target = lax.broadcasted_iota(jnp.int32, (128, pairs * 128), 1)
@@ -119,7 +119,7 @@
         for i in range(frame_count):
             frames_f32[i, :, across] = queue[pl.ds(i * halves * fields + half, fields, halves), :]
         for i in range(steps):
-            noise[i, :, across] = noise_rows[pl.ds(i * halves * fields + half, fields, halves), :]
+            noise[i, :, across] = noise_rows[i, :, 0, across]
     for s in range(steps):
         both = dot_n(noise[s].astype(BF), pick[0] + pick[1])
         noise_edges[me, s] = both.astype(BF)
@@ -349,44 +349,36 @@
         padded[position, :, 2 * width :] = from_east.astype(BF)
 
     def convolve(index):
+        frames = pl.ds(2 * index, 2)
         total = None
         for offset in range(9):
             down, right = offset // 3, offset % 3
-            window = padded[index, down * side : down * side + cells, right * width : (right + 1) * width]
-            product = dot_t(window, conv_weight[offset])
+            window = padded[frames, down * side : down * side + cells, right * width : (right + 1) * width]
+            product = dot_t(window.reshape(2 * cells, width), conv_weight[offset])
             total = product if total is None else total + product
-        centre = padded[index, side : side + cells, width : 2 * width].astype(F32)
-        result = (centre + total / (1.0 + jnp.exp(-total))).astype(BF)
-        hidden[index] = result
+        centre = padded[frames, side : side + cells, width : 2 * width].reshape(2 * cells, width)
+        result = (centre.astype(F32) + total / (1.0 + jnp.exp(-total))).astype(BF)
+        hidden[frames] = result.reshape(2, cells, width)
         widened = result.astype(F32)
         mean = jnp.mean(widened * widened, axis=1, keepdims=True)
         norm = (widened * lax.rsqrt(mean + 1e-06) * norm_gain[...]).astype(BF)
-        memory[index] = dot_t(norm, memory_weight[...]).astype(BF)
-        normed[index] = norm
+        memory[frames] = dot_t(norm, memory_weight[...]).astype(BF).reshape(2, cells, 2 * width)
+        normed[frames] = norm.reshape(2, cells, width)
 
     rows_at_once = 128
 
     def attend(chunk):
         begin = pl.multiple_of(chunk * rows_at_once, rows_at_once)
         here = pl.ds(begin, rows_at_once)
-        lower = lax.broadcasted_iota(jnp.int32, (1, 128), 1) < 64
-        asked = [queries[i, here].astype(F32) for i in range(frame_count)]
-
         def partial(i, j):
-            product = asked[i] * memory[j, here, :width].astype(F32)
+            product = queries[i, here] * memory[j, here, :width]
             total = product[:, :128]
             for start in range(128, width, 128):
                 total = total + product[:, start : start + 128]
             return total
 
         def score_block(first):
-            pieces = []
-            for c in range(pairs // 2):
-                later = c + pairs // 2
-                one = partial(c % frame_count, first + c // frame_count)
-                two = partial(later % frame_count, first + later // frame_count)
-                swapped = pltpu.roll(jnp.where(lower, two, one), 64, 1)
-                pieces.append((jnp.where(lower, one, two) + swapped).astype(BF))
+            pieces = [partial(c % frame_count, first + c // frame_count) for c in range(pairs)]
             return dot_n(jnp.concatenate(pieces, axis=1), head_sum[...]) * head_size ** (-0.5)
 
         near = score_block(0)
@@ -406,12 +398,15 @@
             context = None
             columns = slice(i * frame_count * 128, (i + 1) * frame_count * 128)
             for block, weight in enumerate((near, far)):
-                spread = dot_n(weight, head_spread[:, columns])
+                spread = dot_n(weight, head_spread[:, columns]).astype(BF)
+                some = None
                 for at in range(frame_count):
                     wide = spread[:, at * 128 : (at + 1) * 128]
-                    values = memory[block * frame_count + at, here, width:].astype(F32)
+                    values = memory[block * frame_count + at, here, width:]
                     term = jnp.concatenate([wide] * (width // 128), axis=1) * values
-                    context = term if context is None else context + term
+                    some = term if some is None else some + term
+                some = some.astype(F32)
+                context = some if context is None else context + some
             refined = hidden[i, here].astype(F32) + dot_t(context.astype(BF), attend_out[...])
             projected = dot_t(decode_weight[...], refined.astype(BF))
             sigma = sigma_own[i : i + 1, :rows_at_once]
@@ -443,7 +438,7 @@
             lift(step, position)
         if step == 0:
             load.wait()
-        lax.fori_loop(0, frame_count - 1, lambda index, c: (convolve(index), c)[1], 0)
+        lax.fori_loop(0, half // 2, lambda index, c: (convolve(index), c)[1], 0)
         arrive_next(step, step == 0)
         for pair in range(half, frame_count):
             halo_of(step, pair)
@@ -452,7 +447,7 @@
         arrive_second(step)
         halo_of(step, frame_count)
         lift(step, reach - 1)
-        lax.fori_loop(frame_count - 1, reach, lambda index, c: (convolve(index), c)[1], 0)
+        lax.fori_loop(half // 2, frame_count, lambda index, c: (convolve(index), c)[1], 0)
         for i in range(frame_count):
             queries[i] = dot_t(normed[i], query_weight[...]).astype(BF)
         lax.fori_loop(0, cells // rows_at_once, lambda chunk, c: (attend(chunk), c)[1], 0)
@@ -498,7 +493,7 @@
             pltpu.VMEM((8, 256), F32),
             pltpu.VMEM((8, 256), F32),
             pltpu.VMEM((128, width), BF),
-            pltpu.VMEM((frames * frames * 64, 128), BF),
+            pltpu.VMEM((frames * frames * 128, 128), BF),
             pltpu.VMEM((128, frames * frames * 128), BF),
             pltpu.VMEM((2, cells, 128), BF),
             pltpu.VMEM((2, 128, cells), F32),
@@ -522,7 +517,7 @@
         ),
     )(
         levels, plan, neighbours, queue_state.reshape(-1, 128),
-        fresh_noise.reshape(-1, 128), in_weight.T, level_embed.reshape(1, width),
+        fresh_noise, in_weight.T, level_embed.reshape(1, width),
         conv_weight, norm_gain.reshape(1, width), query_weight, memory_weight, attend_out,
         decode_weight,
     )

time: 51.8 us -> 48.4 us (0.934)
  Pallas kernels: 47.8 us -> 46.3 us
  other arithmetic: 1.25 us -> 0 us
  local copies, waits for them, and re-layouts: 2.53 us -> 1.86 us
    pallas_call x1, Pallas kernels: 47.8 us -> 46.3 us  [shards(): pl.pallas_call(functools.partial(kernel, groups, tiles), out_shape=jax.Sh...]
    unnamed x1 -> x0, other arithmetic: 1.25 us -> none
    reshape x1 -> x0, local copies, waits for them, and re-layouts: 0.67 us -> none  [shards(): fresh_noise.reshape(-1, 128)]
where the time goes in v2:
time: 48.4 us; the launch traced here: 48.2 us
  Pallas kernels  46.3 us (96%)
  local copies, waits for them, and re-layouts  1.86 us (4%)
    pallas_call x1, Pallas kernels, shards(): pl.pallas_call(functools.partial(kernel, groups, tiles), out_shape=jax.Sh...  46.3 us
    unnamed x1, local copies, waits for them, and re-layouts  1.86 us

profile of v2, /device:TPU:0, one launch (start us, length us, event | category | flops | bytes accessed | tf_op | source)
XLA Modules:
  0.0 48.2 jit_solution(12219280976407503144)
XLA Ops:
  0.0 46.3 %shard_map.127 = f32[552,128]{1,0:T(8,128)} custom-call(s32[4]{0:T(128)} %levels.1, f32[17]{0:T(128)} %plan.1, s32[4,4]{1,0:T(4,128)} %neighbours.1, f32[552,128]{1,0:T(8,128)} %bitcast.6, f32[2,69,1,256]{3,2,1,0:T(1,128)} %noise_rows.1, bf16[69,256]{1,0:T(8,128)(2,1)} %bitcast.7, f32[1,256]{1,0:T(1,128)} %bitcast.8, bf16[9,256,256]{2,1,0:T(8,128)(2,1)} %conv_hbm.1, ...), custom_call_target="tpu_custom_call" | custom-call | tf_op jit(solution)/shard_map/pallas_call | solution.py:471
  46.3 1.9 %copy.17 = f32[4,69,1,256]{3,2,1,0:T(1,128)} copy(f32[4,69,1,256]{3,2,1,0:T(1,128)} %bitcast.5) | data formatting | bytes 565248

commit v3 on v2

--- a/solution.py
+++ b/solution.py
@@ -365,7 +365,7 @@
         memory[frames] = dot_t(norm, memory_weight[...]).astype(BF).reshape(2, cells, 2 * width)
         normed[frames] = norm.reshape(2, cells, width)
 
-    rows_at_once = 128
+    rows_at_once = cells
 
     def attend(chunk):
         begin = pl.multiple_of(chunk * rows_at_once, rows_at_once)

time: 48.4 us -> 45 us (0.930)
  Pallas kernels: 46.3 us -> 43 us
    pallas_call x1, Pallas kernels: 46.3 us -> 43 us  [shards(): pl.pallas_call(functools.partial(kernel, groups, tiles), out_shape=jax.Sh...]
where the time goes in v3:
time: 45 us; the launch traced here: 44.8 us
  Pallas kernels  43 us (96%)
  local copies, waits for them, and re-layouts  1.86 us (4%)
    pallas_call x1, Pallas kernels, shards(): pl.pallas_call(functools.partial(kernel, groups, tiles), out_shape=jax.Sh...  43 us
    unnamed x1, local copies, waits for them, and re-layouts  1.86 us

profile of v3, /device:TPU:0, one launch (start us, length us, event | category | flops | bytes accessed | tf_op | source)
XLA Modules:
  0.0 44.8 jit_solution(5454800426676412476)
XLA Ops:
  0.0 43.0 %shard_map.127 = f32[552,128]{1,0:T(8,128)} custom-call(s32[4]{0:T(128)} %levels.1, f32[17]{0:T(128)} %plan.1, s32[4,4]{1,0:T(4,128)} %neighbours.1, f32[552,128]{1,0:T(8,128)} %bitcast.6, f32[2,69,1,256]{3,2,1,0:T(1,128)} %noise_rows.1, bf16[69,256]{1,0:T(8,128)(2,1)} %bitcast.7, f32[1,256]{1,0:T(1,128)} %bitcast.8, bf16[9,256,256]{2,1,0:T(8,128)(2,1)} %conv_hbm.1, ...), custom_call_target="tpu_custom_call" | custom-call | tf_op jit(solution)/shard_map/pallas_call | solution.py:471
  43.0 1.9 %copy.17 = f32[4,69,1,256]{3,2,1,0:T(1,128)} copy(f32[4,69,1,256]{3,2,1,0:T(1,128)} %bitcast.5) | data formatting | bytes 565248
